TPU v7x, 256 devices: a whole 4x4x8 slice. The times are simulated.
256 devices in a mesh: row: 8 (over y, core), col: 32 (over x, z).
Axes of the slice: x: 4, y: 4, z: 8, core: 2. Of those that a mesh axis runs over, the one named last changes fastest.
Arguments:
- adjoint: bfloat16 [16384, 16384], P('row', 'col'), may hold values from -1 to 1, as said below
- taper: int32 [64, 64], replicated, may hold values from 0 to 1, as said below
- panel_two: bfloat16 [16384, 1024], P(('row', 'col')), may hold values from -6 to 6
- panel_one: bfloat16 [16384, 1024], P(('row', 'col')), may hold values from -6 to 6
- incoming: float32 [16384, 1024], P('col', 'row'), may hold values from -6 to 6
- inverse_factor: bfloat16 [1024, 1024], P('row'), may hold values from -1 to 1, as said below
Outputs:
- second_grad: float32 [16384, 1024], P('col', 'row')
- first_grad: float32 [16384, 1024], P('col', 'row')
Inputs may be any that keep to these rules, and one draw needn't show every extreme that they name: `taper`: symmetric in its two indices; every entry with |a - b| <= 1 is 1. `adjoint`: symmetric. `inverse_factor`: lower triangular with a positive diagonal.
All inputs are finite; a program needn't handle non-finite values.
Results may differ from a plain program's by a relative error of at most 0.0025.
Values may be sent and summed in bfloat16 or wider, within the bound.
No kernel may reach another device: no remote copies, remote signals or barrier semaphores. Data moves between devices by JAX's collectives and lax.ppermute only.
A program may use at most 64 MiB of HBM per device.

v0:
```python
import jax
import jax.numpy as jnp
from jax import lax
from jax.sharding import PartitionSpec as P

BLK = 256


def broadcast(value, axis, source):
    kept = jnp.where(lax.axis_index(axis) == source, value, 0).astype(value.dtype)
    return lax.psum(kept, axis)


def mask_tiles(taper, row_tiles, col_tiles):
    first_row = lax.axis_index("row") * row_tiles
    first_col = lax.axis_index("col") * col_tiles
    return lax.dynamic_slice(taper, (first_row, first_col), (row_tiles, col_tiles))


def masked_local(adjoint, mask_block, tile_size):
    row_count, col_count = adjoint.shape
    shaped = adjoint.reshape(row_count // tile_size, tile_size, col_count // tile_size, tile_size)
    keep_mask = mask_block.astype(adjoint.dtype)[:, None, :, None]
    return (shaped * keep_mask).reshape(row_count, col_count)


def local(adjoint, taper, panel_two, panel_one, incoming, inverse_factor):
    tile_size = BLK
    row_tiles = adjoint.shape[0] // tile_size
    col_tiles = adjoint.shape[1] // tile_size
    mask_block = mask_tiles(taper, row_tiles, col_tiles)

    def gather_rows(panel):
        return lax.all_gather(panel, "col", axis=0, tiled=True)

    def spread(mirror_term):
        return lax.psum_scatter(mirror_term, "row", scatter_dimension=1, tiled=True)

    masked = masked_local(adjoint, mask_block, tile_size)

    def mirror(gathered):
        return lax.dot_general(
            masked, gathered, (((0,), (0,)), ((), ())), preferred_element_type=jnp.float32
        )

    rows_second = gather_rows(panel_two)
    second_grad = incoming + spread(-2.0 * mirror(rows_second))
    second_rounded = second_grad.astype(jnp.bfloat16)
    rows_first = gather_rows(panel_one)
    panel_width = panel_one.shape[1]
    diagonal_block = broadcast(rows_first[:panel_width], "row", 0)
    first_term = -2.0 * mirror(rows_first)
    partial_value = jnp.dot(second_rounded, inverse_factor, preferred_element_type=jnp.float32)
    carried = lax.psum(partial_value, "row")
    slab_rows = inverse_factor.shape[0]
    columns = lax.dynamic_slice_in_dim(
        diagonal_block, lax.axis_index("row") * slab_rows, slab_rows, 1
    ).astype(jnp.float32)
    carried_term = jnp.dot(
        carried, columns, precision=lax.Precision.HIGHEST, preferred_element_type=jnp.float32
    )
    first_grad = spread(first_term) - carried_term
    return (second_grad, first_grad)


def solution(mesh):
    in_specs = (
        P("row", "col"),
        P(),
        P(("row", "col"), None),
        P(("row", "col"), None),
        P("col", "row"),
        P("row", None),
    )
    out_specs = (P("col", "row"), P("col", "row"))
    return jax.shard_map(local, mesh=mesh, in_specs=in_specs, out_specs=out_specs, check_vma=False)
```

profile of v0, /device:TPU:2, one launch (start us, length us, event | category | flops | bytes accessed | tf_op | source)
XLA Modules:
  0.0 405.2 jit_solution(9717838235637787397)
XLA Ops:
  7.2 0.0 all-gather.3.cloned.1.call-start
  7.2 0.7 all-gather.3.cloned.1.call-update
  7.9 0.0 all-gather.5.cloned.1.call-start
  8.0 0.7 all-gather.5.cloned.1.call-update
  8.7 0.0 reduce-scatter.3.cloned.1.call-start
  8.7 0.8 dynamic-slice_convert_fusion
  9.5 1.1 mul.28
  10.6 0.5 copy.8
  11.1 82.9 %all-gather.3.cloned.1.call-done = bf16[2048,1024]{1,0:T(8,128)(2,1)} async-done(((bf16[64,1024]{1,0:T(8,128)(2,1)}), bf16[2048,1024]{1,0:T(8,128)(2,1)}) %all-gather.3.cloned.1.call-update) | async-done | bytes 4194320 | tf_op jit(solution)/shard_map/all_gather | solution.py:34
  94.1 6.5 %convolution_multiply_fusion.1 = f32[512,1024]{1,0:T(8,128)} fusion(bf16[2048,1024]{1,0:T(8,128)(2,1)} %all-gather.3.cloned.1.call-done, bf16[2048,512]{1,0:T(8,128)(2,1)} %param.6, bf16[2048,512]{1,0:T(8,128)(2,1)S(1)} %bitcast.8), kind=kOutput, calls=%fused_computation.2 | convolution fusion | flops 2149056512 | bytes 10485760 | tf_op jit(solution)/shard_map/dot_general | solution.py:42
  100.6 0.0 reduce-scatter.3.cloned.1.call-update
  100.6 0.0 all-reduce.5.cloned.1.call-start
  100.7 75.0 %all-gather.5.cloned.1.call-done = bf16[2048,1024]{1,0:T(8,128)(2,1)} async-done(((bf16[64,1024]{1,0:T(8,128)(2,1)}), bf16[2048,1024]{1,0:T(8,128)(2,1)}) %all-gather.5.cloned.1.call-update) | async-done | bytes 4194320 | tf_op jit(solution)/shard_map/all_gather | solution.py:34
  175.7 3.1 slice_select_fusion
  178.8 0.0 reduce-scatter.5.cloned.1.call-start
  178.9 6.5 %convolution_multiply_fusion = f32[512,1024]{1,0:T(8,128)} fusion(bf16[2048,1024]{1,0:T(8,128)(2,1)} %all-gather.5.cloned.1.call-done, bf16[2048,512]{1,0:T(8,128)(2,1)} %param.6, bf16[2048,512]{1,0:T(8,128)(2,1)S(1)} %bitcast.9), kind=kOutput, calls=%fused_computation.1 | convolution fusion | flops 2149056512 | bytes 10485760 | tf_op jit(solution)/shard_map/dot_general | solution.py:42
  185.4 0.0 all-reduce.3.cloned.1.call-start
  185.5 27.6 %reduce-scatter.3.cloned.1.call-done = f32[512,128]{1,0:T(8,128)} async-done(((f32[512,1024]{1,0:T(8,128)}), f32[512,128]{1,0:T(8,128)}) %reduce-scatter.3.cloned.1.call-update) | async-done | bytes 262160 | tf_op jit(solution)/shard_map/reduce_scatter | solution.py:37
  213.0 1.0 add.22
  214.0 1.8 fusion.3
  215.8 69.0 %all-reduce.5.cloned.1.call-done = bf16[1024,1024]{1,0:T(8,128)(2,1)} async-done(((bf16[1024,1024]{1,0:T(8,128)(2,1)}), bf16[1024,1024]{1,0:T(8,128)(2,1)}) %all-reduce.5.cloned.1.call-update) | async-done | bytes 2097168 | tf_op jit(solution)/shard_map/psum | solution.py:11
  284.9 38.1 %reduce-scatter.5.cloned.1.call-done = f32[512,128]{1,0:T(8,128)} async-done(((f32[512,1024]{1,0:T(8,128)}), f32[512,128]{1,0:T(8,128)}) %reduce-scatter.5.cloned.1.call-update) | async-done | bytes 262160 | tf_op jit(solution)/shard_map/reduce_scatter | solution.py:37
  323.0 71.9 %all-reduce.3.cloned.1.call-done = f32[512,1024]{1,0:T(8,128)} async-done(((f32[512,1024]{1,0:T(8,128)}), f32[512,1024]{1,0:T(8,128)}) %all-reduce.3.cloned.1.call-update) | async-done | bytes 2097168 | tf_op jit(solution)/shard_map/psum | solution.py:54
  394.9 3.4 convolution_subtract_fusion
  (9 shorter events, 0.1 us)
Async XLA Ops:
  7.2 206.8 %copy-start = (bf16[128,1024]{1,0:T(8,128)(2,1)S(1)}, bf16[128,1024]{1,0:T(8,128)(2,1)}, u32[]{:S(2)}) copy-start(bf16[128,1024]{1,0:T(8,128)(2,1)} %param.11) | copy-start | bytes 786436
  7.2 86.9 %all-gather.3.cloned.1.call-start = ((), (), s32[]{:S(2)}) async-start(), calls=%async_computation.2 | async-start | bytes 4325376 | tf_op jit(solution)/shard_map/all_gather | solution.py:34
  7.9 167.8 %all-gather.5.cloned.1.call-start = ((), (), s32[]{:S(2)}) async-start(), calls=%async_computation.4 | async-start | bytes 4325376 | tf_op jit(solution)/shard_map/all_gather | solution.py:34
  8.7 204.4 %reduce-scatter.3.cloned.1.call-start = ((), (), s32[]{:S(2)}) async-start(), calls=%async_computation.3 | async-start | bytes 2359296 | tf_op jit(solution)/shard_map/reduce_scatter | solution.py:37
  100.6 184.2 %all-reduce.5.cloned.1.call-start = ((), (), s32[]{:S(2)}) async-start(), calls=%async_computation.7 | async-start | bytes 4194304 | tf_op jit(solution)/shard_map/psum | solution.py:11
  178.8 144.2 %reduce-scatter.5.cloned.1.call-start = ((), (), s32[]{:S(2)}) async-start(), calls=%async_computation.5 | async-start | bytes 2359296 | tf_op jit(solution)/shard_map/reduce_scatter | solution.py:37
  185.4 27.7 %copy-start.2 = (f32[512,128]{1,0:T(8,128)S(1)}, f32[512,128]{1,0:T(8,128)}, u32[]{:S(2)}) copy-start(f32[512,128]{1,0:T(8,128)} %param.10) | copy-start | bytes 786436
  185.4 209.5 %all-reduce.3.cloned.1.call-start = ((), (), s32[]{:S(2)}) async-start(), calls=%async_computation.6 | async-start | bytes 4194304 | tf_op jit(solution)/shard_map/psum | solution.py:54
  214.0 1.8 copy-start.1
Sparse Core Ops, SparseCore 0:
  10.6 83.4 all-gather.2
  96.7 78.9 all-gather.4
  178.3 34.7 reduce-scatter.2
  215.2 69.5 all-reduce.4
  287.3 35.6 reduce-scatter.4
  325.2 69.6 all-reduce.2
where the time goes:
time: 405 us
  waiting for transfers between devices  366 us (90%)
  matrix products  18.3 us (5%)
  between operations  14.2 us (4%)
  other arithmetic  4.82 us (1%)
    all_gather x2, waiting for transfers between devices, gather_rows(): return lax.all_gather(panel, 'col', axis=0, tiled=True)  158 us
    psum x1, waiting for transfers between devices, local(): carried = lax.psum(partial_value, 'row')  71.9 us
    psum x1, waiting for transfers between devices, broadcast(): return lax.psum(kept, axis)  69 us
    reduce_scatter x2, waiting for transfers between devices, spread(): return lax.psum_scatter(mirror_term, 'row', scatter_dimension=1, tiled=True)  65.7 us
    dot_general x2, matrix products, mirror(): lax.dot_general(masked, gathered, (((0,), (0,)), ((), ())), preferred_ele...  13.1 us
  transfers between devices with their start and end apart: 6, of which 6 were waited for; matrix products, arithmetic and copies ran while one was open for 5% of the time, Pallas kernels for 0%

commit v1 on v0

--- a/solution.py
+++ b/solution.py
@@ -2,6 +2,7 @@
 import jax.numpy as jnp
 from jax import lax
 from jax.sharding import PartitionSpec as P
+from jax.lax import all_gather
 
 BLK = 256
 
@@ -51,7 +52,8 @@
     diagonal_block = broadcast(rows_first[:panel_width], "row", 0)
     first_term = -2.0 * mirror(rows_first)
     partial_value = jnp.dot(second_rounded, inverse_factor, preferred_element_type=jnp.float32)
-    carried = lax.psum(partial_value, "row")
+    drive_plate = lambda view: jnp.sum(all_gather(view, axis_name="row"), 0)
+    carried = drive_plate(partial_value)
     slab_rows = inverse_factor.shape[0]
     columns = lax.dynamic_slice_in_dim(
         diagonal_block, lax.axis_index("row") * slab_rows, slab_rows, 1

time: 405 us -> 427 us (1.054)
  waiting for transfers between devices: 366 us -> 380 us
  other arithmetic: 4.82 us -> 12.8 us
    all_gather x0 -> x1, waiting for transfers between devices: none -> 78.1 us  [local(): drive_plate = lambda view: jnp.sum(all_gather(view, axis_name='row'), 0)]
    psum x1 -> x0, waiting for transfers between devices: 71.9 us -> none  [local(): carried = lax.psum(partial_value, 'row')]
    reduce_sum x0 -> x1, other arithmetic: none -> 7.96 us  [local(): drive_plate = lambda view: jnp.sum(all_gather(view, axis_name='row'), 0)]
    reduce_scatter x2, waiting for transfers between devices: 65.7 us -> 72.2 us  [spread(): return lax.psum_scatter(mirror_term, 'row', scatter_dimension=1, tiled=True)]
    all_gather x2, waiting for transfers between devices: 158 us -> 163 us  [gather_rows(): return lax.all_gather(panel, 'col', axis=0, tiled=True)]
where the time goes in v1:
time: 427 us
  waiting for transfers between devices  380 us (89%)
  matrix products  17.6 us (4%)
  between operations  14.2 us (3%)
  other arithmetic  12.8 us (3%)
    all_gather x2, waiting for transfers between devices, gather_rows(): return lax.all_gather(panel, 'col', axis=0, tiled=True)  163 us
    all_gather x1, waiting for transfers between devices, local(): drive_plate = lambda view: jnp.sum(all_gather(view, axis_name='row'), 0)  78.1 us
    reduce_scatter x2, waiting for transfers between devices, spread(): return lax.psum_scatter(mirror_term, 'row', scatter_dimension=1, tiled=True)  72.2 us
    psum x1, waiting for transfers between devices, broadcast(): return lax.psum(kept, axis)  65.7 us
    dot_general x2, matrix products, mirror(): lax.dot_general(masked, gathered, (((0,), (0,)), ((), ())), preferred_ele...  13 us
  transfers between devices with their start and end apart: 6, of which 6 were waited for; matrix products, arithmetic and copies ran while one was open for 5% of the time, Pallas kernels for 0%

profile of v1, /device:TPU:2, one launch (start us, length us, event | category | flops | bytes accessed | tf_op | source)
XLA Modules:
  0.0 426.7 jit_solution(10190039708352052983)
XLA Ops:
  7.2 0.0 all-gather.5.cloned.1.call-start
  7.2 0.7 all-gather.5.cloned.1.call-update
  7.9 0.0 reduce-scatter.3.cloned.1.call-start
  8.0 0.8 dynamic-slice_convert_fusion
  8.7 1.1 mul.28
  9.9 0.5 copy.8
  10.4 83.7 %all-gather.5.cloned.1.call-done = bf16[2048,1024]{1,0:T(8,128)(2,1)} async-done(((bf16[64,1024]{1,0:T(8,128)(2,1)}), bf16[2048,1024]{1,0:T(8,128)(2,1)}) %all-gather.5.cloned.1.call-update) | async-done | bytes 4194320 | tf_op jit(solution)/shard_map/all_gather | solution.py:35
  94.1 6.5 %convolution_multiply_fusion.1 = f32[512,1024]{1,0:T(8,128)} fusion(bf16[2048,1024]{1,0:T(8,128)(2,1)} %all-gather.5.cloned.1.call-done, bf16[2048,512]{1,0:T(8,128)(2,1)} %param.6, bf16[2048,512]{1,0:T(8,128)(2,1)S(1)} %bitcast.10), kind=kOutput, calls=%fused_computation.2 | convolution fusion | flops 2149056512 | bytes 10485760 | tf_op jit(solution)/shard_map/dot_general | solution.py:43
  100.6 0.0 all-gather.7.cloned.1.call-start
  100.7 0.7 all-gather.7.cloned.1.call-update
  101.3 0.0 all-gather.9.cloned.1.call-start
  101.4 34.1 %reduce-scatter.3.cloned.1.call-done = f32[512,128]{1,0:T(8,128)} async-done(((f32[512,1024]{1,0:T(8,128)}), f32[512,128]{1,0:T(8,128)}) %reduce-scatter.3.cloned.1.call-update) | async-done | bytes 262160 | tf_op jit(solution)/shard_map/reduce_scatter | solution.py:38
  135.5 1.0 add.20
  136.5 1.8 fusion.3
  138.3 0.0 all-reduce.2.cloned.1.call-start
  138.4 79.0 %all-gather.7.cloned.1.call-done = bf16[2048,1024]{1,0:T(8,128)(2,1)} async-done(((bf16[64,1024]{1,0:T(8,128)(2,1)}), bf16[2048,1024]{1,0:T(8,128)(2,1)}) %all-gather.7.cloned.1.call-update) | async-done | bytes 4194320 | tf_op jit(solution)/shard_map/all_gather | solution.py:35
  217.4 3.1 slice_select_fusion
  220.5 0.0 reduce-scatter.5.cloned.1.call-start
  220.6 6.5 %convolution_multiply_fusion = f32[512,1024]{1,0:T(8,128)} fusion(bf16[2048,1024]{1,0:T(8,128)(2,1)} %all-gather.7.cloned.1.call-done, bf16[2048,512]{1,0:T(8,128)(2,1)} %param.6, bf16[2048,512]{1,0:T(8,128)(2,1)S(1)} %bitcast.11), kind=kOutput, calls=%fused_computation.1 | convolution fusion | flops 2149056512 | bytes 10485760 | tf_op jit(solution)/shard_map/dot_general | solution.py:43
  227.1 78.1 %all-gather.9.cloned.1.call-done = f32[4096,1024]{1,0:T(8,128)} async-done(((f32[512,1024]{1,0:T(8,128)}), f32[4096,1024]{1,0:T(8,128)}) %all-gather.9.cloned.1.call-update) | async-done | bytes 16777232 | tf_op jit(solution)/shard_map/all_gather | solution.py:55
  305.2 8.0 %reduce_sum.9 = f32[512,1024]{1,0:T(8,128)S(1)} reduce(f32[8,512,1024]{2,1,0:T(8,128)} %bitcast.8, f32[]{:T(128)} %constant.23.clone.1), dimensions={0}, to_apply=%region_2.3 | reduce | flops 3670016 | bytes 18874372 | tf_op jit(solution)/shard_map/reduce_sum | solution.py:55
  313.2 65.7 %all-reduce.2.cloned.1.call-done = bf16[1024,1024]{1,0:T(8,128)(2,1)} async-done(((bf16[1024,1024]{1,0:T(8,128)(2,1)}), bf16[1024,1024]{1,0:T(8,128)(2,1)}) %all-reduce.2.cloned.1.call-update) | async-done | bytes 2097168 | tf_op jit(solution)/shard_map/psum | solution.py:12
  378.9 38.1 %reduce-scatter.5.cloned.1.call-done = f32[512,128]{1,0:T(8,128)} async-done(((f32[512,1024]{1,0:T(8,128)}), f32[512,128]{1,0:T(8,128)}) %reduce-scatter.5.cloned.1.call-update) | async-done | bytes 262160 | tf_op jit(solution)/shard_map/reduce_scatter | solution.py:38
  417.0 2.8 convolution_subtract_fusion
  (10 shorter events, 0.1 us)
Async XLA Ops:
  7.2 129.3 %copy-start = (bf16[128,1024]{1,0:T(8,128)(2,1)S(1)}, bf16[128,1024]{1,0:T(8,128)(2,1)}, u32[]{:S(2)}) copy-start(bf16[128,1024]{1,0:T(8,128)(2,1)} %param.11) | copy-start | bytes 786436
  7.2 86.9 %all-gather.5.cloned.1.call-start = ((), (), s32[]{:S(2)}) async-start(), calls=%async_computation.2 | async-start | bytes 4325376 | tf_op jit(solution)/shard_map/all_gather | solution.py:35
  7.9 127.6 %reduce-scatter.3.cloned.1.call-start = ((), (), s32[]{:S(2)}) async-start(), calls=%async_computation.3 | async-start | bytes 2359296 | tf_op jit(solution)/shard_map/reduce_scatter | solution.py:38
  100.6 34.9 %copy-start.2 = (f32[512,128]{1,0:T(8,128)S(1)}, f32[512,128]{1,0:T(8,128)}, u32[]{:S(2)}) copy-start(f32[512,128]{1,0:T(8,128)} %param.10) | copy-start | bytes 786436
  100.6 116.8 %all-gather.7.cloned.1.call-start = ((), (), s32[]{:S(2)}) async-start(), calls=%async_computation.4 | async-start | bytes 4325376 | tf_op jit(solution)/shard_map/all_gather | solution.py:35
  101.3 203.9 %all-gather.9.cloned.1.call-start = ((), (), s32[]{:S(2)}) async-start(), calls=%async_computation.7 | async-start | bytes 18874368 | tf_op jit(solution)/shard_map/all_gather | solution.py:55
  136.5 1.8 copy-start.1
  138.3 240.6 %all-reduce.2.cloned.1.call-start = ((), (), s32[]{:S(2)}) async-start(), calls=%async_computation.6 | async-start | bytes 4194304 | tf_op jit(solution)/shard_map/psum | solution.py:12
  220.5 196.5 %reduce-scatter.5.cloned.1.call-start = ((), (), s32[]{:S(2)}) async-start(), calls=%async_computation.5 | async-start | bytes 2359296 | tf_op jit(solution)/shard_map/reduce_scatter | solution.py:38
Sparse Core Ops, SparseCore 0:
  10.6 83.4 all-gather.4
  100.7 34.7 reduce-scatter.2
  138.1 79.2 all-gather.6
  219.1 86.0 all-gather.8
  307.4 71.4 all-reduce.1
  381.3 35.6 reduce-scatter.4
